TPU v7x, 512 devices: a whole 4x8x8 slice. The times are simulated.
512 devices in a mesh: seq: 16 (over y, core), kv: 8 (over z), dp: 4 (over x).
Axes of the slice: x: 4, y: 8, z: 8, core: 2. Of those that a mesh axis runs over, the one named last changes fastest.
Arguments:
- queries: bfloat16 [65536, 2048], P(('dp', 'seq', 'kv')), parts along dimension 0, may hold values from -9 to 9
- keys: bfloat16 [65536, 512], P(('dp', 'seq', 'kv')), parts along dimension 0, may hold values from -4 to 4
- values: bfloat16 [65536, 512], P(('dp', 'seq', 'kv')), parts along dimension 0, may hold values from -6 to 6
- doc_ids: int32 [65536], P(('dp', 'seq', 'kv')), parts along dimension 0, may hold values from 0 to 7, never falling along the last dimension, each value on 1 to 4096 neighbouring positions
- beta: float32 [16], replicated, may hold values from -2 to 2
- lin_gain: float32 [2048], replicated, may hold values from 0.1 to 1.9
Outputs:
- mixed: float32 [65536, 2048], P(('dp', 'seq', 'kv')), parts along dimension 0
There are 4 independent parts, one for each index of `dp`. A program takes and returns all parts, laid end to end along the dimension named above; an argument that names none is the same for every part. Nothing has to cross between parts.
Inputs may be any that keep to these rules, and one draw needn't show every extreme that they name: `doc_ids`: document ids never fall along a packed sequence; each document holds 1 to 4096 tokens.
All inputs are finite; a program needn't handle non-finite values.
Results may differ from a plain program's by a relative error of at most 0.0012.
Values may be sent and summed in bfloat16 or wider, within the bound.
A program may use at most 64 MiB of HBM per device.

v0:
```python
import jax
import jax.numpy as jnp
from jax import lax
from jax.sharding import Mesh
from jax.sharding import PartitionSpec as P

HEADS = 16
KV_HEADS = 4
HEAD_DIM = 128
SEQ = ("seq_0", "seq_1")
DP_SEQ_KV = ("dp", "seq_0", "seq_1", "kv")


def in_one_piece(arrays, axis, dim, along):
    widths = [a.shape[along] for a in arrays]
    both = jnp.concatenate(arrays, axis=along)
    out = lax.all_gather(both, axis, axis=dim, tiled=True)
    return tuple(jnp.split(out, [sum(widths[:k]) for k in range(1, len(widths))], axis=along))


def nothing_yet(x, identity):
    return jax.tree.map(
        lambda part, zero: jnp.zeros_like(part) + jnp.asarray(zero, part.dtype), x, identity
    )


def all_in_one(x, axis):
    leaves = jax.tree.leaves(x)
    order = sorted(range(len(leaves)), key=lambda k: -leaves[k].size)
    width = (1, *leaves[order[0]].shape)[-1]
    lines = [
        jnp.pad(leaves[k].reshape(-1), (0, -leaves[k].size % width)).reshape(-1, width)
        for k in order
    ]
    both, at, found = (lax.all_gather(jnp.concatenate(lines), axis), 0, {})
    for k, line in zip(order, lines):
        section = both[:, at : at + len(line)].reshape(len(both), -1)
        found[k] = section[:, : leaves[k].size].reshape(-1, *leaves[k].shape)
        at += len(line)
    numbers = iter(range(len(leaves)))
    return jax.tree.map(lambda _: found[next(numbers)], x)


def collected_alike(x, axis):
    leaves, found = (jax.tree.leaves(x), {})
    for initial, a in enumerate(leaves):
        if initial not in found:
            alike = [k for k, b in enumerate(leaves) if b.dtype == a.dtype]
            got = (
                all_in_one([leaves[k] for k in alike], axis)
                if len(alike) > 1
                else [lax.all_gather(a, axis)]
            )
            for k, b in zip(alike, got):
                found[k] = b
    numbers = iter(range(len(leaves)))
    return jax.tree.map(lambda _: found[next(numbers)], x)


def prefix_by_axis(x, axes, combine, identity):
    before = start = nothing_yet(x, identity)
    so_far = x
    for axis in reversed(axes):
        size, here = (lax.axis_size(axis), lax.axis_index(axis))
        pieces = collected_alike(so_far, axis)
        inside, so_far = (start, start)
        for k in range(size):
            passed = k < here
            so_far = combine(so_far, jax.tree.map(lambda part: part[k], pieces))
            inside = jax.tree.map(lambda new, old: jnp.where(passed, new, old), so_far, inside)
        before = combine(inside, before)
    return before


def join_states(earlier, later):
    state_early, first_early, last_early = earlier
    state_late, first_late, last_late = later
    empty_late = first_late < 0
    joined = (first_late == last_late) & (last_early == first_late)
    merged = state_late + jnp.where(joined, state_early, jnp.zeros_like(state_early))
    combined = jnp.where(empty_late, state_early, merged)
    first_doc = jnp.where(first_early < 0, first_late, first_early)
    last_doc = jnp.where(empty_late, last_early, last_late)
    return (combined, first_doc, last_doc)


def tail_merge(one_side, other_side):
    state_one, first_one, last_one = one_side
    state_other, first_other, last_other = other_side
    top_doc = jnp.maximum(last_one, last_other)
    state_sum = jnp.where(last_one == top_doc, state_one, jnp.zeros_like(state_one))
    state_sum = state_sum + jnp.where(
        last_other == top_doc, state_other, jnp.zeros_like(state_other)
    )
    return (state_sum, jnp.minimum(first_one, first_other), top_doc)


def tail_state(key_rows, value_rows, doc_rows, target_doc):
    count = key_rows.shape[0]
    key_heads = key_rows.reshape(count, KV_HEADS, HEAD_DIM)
    value_heads = value_rows.reshape(count, KV_HEADS, HEAD_DIM)
    live = doc_rows == target_doc
    masked = jnp.where(live[:, None, None], key_heads, jnp.zeros_like(key_heads))
    return jnp.einsum("rgd,rge->gde", masked, value_heads, preferred_element_type=jnp.float32)


def attend_block(
    carry, query_heads, query_pos, query_doc, key_rows, value_rows, key_doc, key_start
):
    running_max, running_sum, accumulated = carry
    key_count = key_rows.shape[0]
    key_heads = key_rows.reshape(key_count, KV_HEADS, HEAD_DIM)
    value_heads = value_rows.reshape(key_count, KV_HEADS, HEAD_DIM)
    scores = jnp.einsum(
        "rgqd,kgd->gqrk", query_heads, key_heads, preferred_element_type=jnp.float32
    )
    scores = scores / jnp.sqrt(jnp.float32(HEAD_DIM))
    key_pos = key_start + jnp.arange(key_count, dtype=jnp.int32)
    allowed = (key_pos[None, :] <= query_pos[:, None]) & (key_doc[None, :] == query_doc[:, None])
    masked = jnp.where(allowed, scores, jnp.float32(-1e30))
    new_max = jnp.maximum(running_max, jnp.max(masked, axis=-1))
    factor = jnp.exp(running_max - new_max)
    weights = jnp.where(allowed, jnp.exp(masked - new_max[..., None]), jnp.float32(0.0))
    new_sum = running_sum * factor + jnp.sum(weights, axis=-1)
    product = jnp.einsum(
        "gqrk,kge->gqre",
        weights.astype(jnp.bfloat16),
        value_heads,
        preferred_element_type=jnp.float32,
    )
    new_accum = accumulated * factor[..., None] + product
    return (new_max, new_sum, new_accum)


def on_device(queries, keys, values, doc_ids, beta, lin_gain):
    row_count = queries.shape[0]
    groups = HEADS // KV_HEADS
    query_heads = queries.reshape(row_count, KV_HEADS, groups, HEAD_DIM)
    position = lax.axis_index("kv") * row_count
    query_pos = position + jnp.arange(row_count, dtype=jnp.int32)
    last_query = position + row_count - 1
    initial = (
        jnp.full((KV_HEADS, groups, row_count), -1e30, jnp.float32),
        jnp.zeros((KV_HEADS, groups, row_count), jnp.float32),
        jnp.zeros((KV_HEADS, groups, row_count, HEAD_DIM), jnp.float32),
    )
    empty_tail = (
        jnp.zeros((KV_HEADS, HEAD_DIM, HEAD_DIM), jnp.float32),
        jnp.array(2**30, jnp.int32),
        jnp.array(-1, jnp.int32),
    )
    key_piece, value_piece, doc_piece = (
        *in_one_piece((keys, values), "kv", 0, 1),
        lax.all_gather(doc_ids, "kv", axis=0, tiled=True),
    )
    blocks = key_piece.shape[0] // row_count

    def one_block(state, item):
        soft_state, tail_now = state
        key_block, value_block, doc_block, number = item
        block_start = number * row_count
        soft_next = lax.cond(
            block_start <= last_query,
            lambda inner: attend_block(
                inner,
                query_heads,
                query_pos,
                doc_ids,
                key_block,
                value_block,
                doc_block,
                block_start,
            ),
            lambda inner: inner,
            soft_state,
        )
        block_tail = (
            tail_state(key_block, value_block, doc_block, doc_block[-1]),
            doc_block[0],
            doc_block[-1],
        )
        tail_now = tail_merge(tail_now, block_tail)
        return ((soft_next, tail_now), None)

    stacked = (
        key_piece.reshape(blocks, row_count, -1),
        value_piece.reshape(blocks, row_count, -1),
        doc_piece.reshape(blocks, row_count),
        jnp.arange(blocks, dtype=jnp.int32),
    )
    result, _ = lax.scan(one_block, (initial, empty_tail), stacked)
    running, segment_tail = result
    running_max, running_sum, accumulated = running
    soft_out = jnp.transpose(accumulated / running_sum[..., None], (2, 0, 1, 3))
    identity = (
        jnp.zeros((KV_HEADS, HEAD_DIM, HEAD_DIM), jnp.float32),
        jnp.array(-1, jnp.int32),
        jnp.array(-1, jnp.int32),
    )
    memory = prefix_by_axis(segment_tail, SEQ, join_states, identity)
    memory_state, memory_first, memory_last = memory
    query_float = query_heads.astype(jnp.float32)
    recalled = jnp.einsum(
        "rgqd,gde->rgqe", query_float, memory_state, precision=lax.Precision.HIGHEST
    )
    recalled = jnp.where((doc_ids == memory_last)[:, None, None, None], recalled, jnp.float32(0.0))
    mean_square = jnp.mean(recalled * recalled, axis=-1, keepdims=True)
    normed = (
        recalled * lax.rsqrt(mean_square + 1e-06) * lin_gain.reshape(KV_HEADS, groups, HEAD_DIM)
    )
    mixing = jax.nn.sigmoid(beta).reshape(KV_HEADS, groups)[None, :, :, None]
    mixed = mixing * normed + (1.0 - mixing) * soft_out
    return mixed.reshape(row_count, HEADS * HEAD_DIM).astype(jnp.float32)


def solution(mesh):
    split = Mesh(
        mesh.devices.reshape(8, 2, mesh.shape["kv"], mesh.shape["dp"]),
        ("seq_0", "seq_1", "kv", "dp"),
    )
    in_specs = (P(DP_SEQ_KV, None), P(DP_SEQ_KV, None), P(DP_SEQ_KV, None), P(DP_SEQ_KV), P(), P())
    out_specs = P(DP_SEQ_KV, None)
    return jax.shard_map(
        on_device, mesh=split, in_specs=in_specs, out_specs=out_specs, check_vma=False
    )
```

profile of v0, /device:TPU:2, one launch (start us, length us, event | category | flops | bytes accessed | tf_op | source)
XLA Modules:
  0.0 181.8 jit_solution(15142142390558384804)
XLA Ops:
  6.5 1.7 pad_maximum_fusion
  8.3 1.3 copy.45
  10.0 1.3 dynamic-slice
  11.9 22.2 %all-gather.3 = s32[8,1,128]{2,1,0:T(1,128)S(1)} all-gather(s32[1,1,128]{2,1,0:T(1,128)S(1)} %bitcast.210), channel_id=1, replica_groups=mesh['seq_0'=8,'seq_1'=2,'kv'=8,'dp'=4] {'kv'}, dimensions={0}, use_global_device_ids=true | all-gather | bytes 4608 | tf_op jit(solution)/shard_map/all_gather | solution.py:154
  34.1 24.7 %all-gather.7.cloned.1.call-done = bf16[1024,1024]{1,0:T(8,128)(2,1)} async-done(((bf16[128,1024]{1,0:T(8,128)(2,1)}), bf16[1024,1024]{1,0:T(8,128)(2,1)}) %all-gather.7.cloned.1.call-update) | async-done | bytes 2097168 | tf_op jit(solution)/shard_map/all_gather | solution.py:17
  58.8 2.6 %fusion.103 = (bf16[1024,512]{1,0:T(8,128)(2,1)S(1)}, bf16[1024,512]{1,0:T(8,128)(2,1)}) fusion(bf16[1024,1024]{1,0:T(8,128)(2,1)} %all-gather.7.cloned.1.call-done), kind=kLoop, calls=%fused_computation.128 | loop fusion | bytes 4194304 | tf_op jit(solution)/shard_map/split | solution.py:18
  61.5 48.8 %while.21 = (s32[]{:T(128)}, f32[4,4,128]{2,1,0:T(4,128)S(1)}, f32[4,4,128]{2,1,0:T(4,128)S(1)}, f32[4,4,128,128]{3,2,1,0:T(8,128)S(1)}, f32[4,128,128]{2,1,0:T(...) while((s32[]{:T(128)}, f32[4,4,128]{2,1,0:T(4,128)S(1)}, ...), condition=%wide.region_5.6_spmd.clone, body=%wide.region_0.5_spmd.clone.sunk | while | flops 154259840 | bytes 8067273 | solution.py:191
  61.6 0.6 dynamic_slice.31
  62.8 0.9 constant_dynamic-slice_fusion.6
  64.0 1.5 conditional.3
  64.8 0.7 convolution_add_fusion
  65.5 0.6 fusion.117
  66.1 0.6 compare_bitcast_fusion.2
  68.9 0.6 dynamic_slice.31
  70.2 0.9 constant_dynamic-slice_fusion.6
  71.4 0.6 fusion.117
  72.0 0.6 compare_bitcast_fusion.2
  74.8 0.6 dynamic_slice.31
  76.1 0.9 constant_dynamic-slice_fusion.6
  77.3 0.6 fusion.117
  77.9 0.6 compare_bitcast_fusion.2
  80.7 0.6 dynamic_slice.31
  82.0 0.9 constant_dynamic-slice_fusion.6
  83.2 0.6 fusion.117
  83.9 0.6 compare_bitcast_fusion.2
  86.7 0.6 dynamic_slice.31
  87.9 0.9 constant_dynamic-slice_fusion.6
  89.2 0.6 fusion.117
  89.8 0.6 compare_bitcast_fusion.2
  92.6 0.6 dynamic_slice.31
  93.8 0.9 constant_dynamic-slice_fusion.6
  95.7 0.6 compare_bitcast_fusion.2
  98.5 0.6 dynamic_slice.31
  99.8 0.9 constant_dynamic-slice_fusion.6
  101.6 0.6 compare_bitcast_fusion.2
  104.4 0.6 dynamic_slice.31
  105.7 0.9 constant_dynamic-slice_fusion.6
  107.5 0.6 compare_bitcast_fusion.2
  110.5 2.3 %all-gather.2 = f32[8,128,128]{2,1,0:T(8,128)S(1)} all-gather(f32[4,128,128]{2,1,0:T(8,128)S(1)} %get-tuple-element.130), channel_id=4, replica_groups=mesh['seq_0'=8,'seq_1'=2,'kv'=8,'dp'=4] {'seq_1'}, dimensions={0}, use_global_device_ids=true | all-gather | bytes 786432 | tf_op jit(solution)/shard_map/all_gather | solution.py:52
  112.8 1.8 all-reduce
  114.7 0.7 fusion.105
  119.2 0.7 fusion.34
  120.0 1.2 dynamic-slice.1
  124.9 13.5 %all-reduce.1 = s32[16]{0:T(128)S(1)} all-reduce(s32[16]{0:T(128)S(1)} %fusion.99), channel_id=3, replica_groups=mesh['seq_0'=8,'seq_1'=2,'kv'=8,'dp'=4] {'seq_0'}, use_global_device_ids=true, to_apply=%add.1 | all-reduce | flops 16 | bytes 128
  138.5 0.7 fusion.104
  161.4 9.1 %all-gather.9.cloned.1.call-done = f32[8,4,128,128]{3,2,1,0:T(8,128)} async-done(((f32[1,4,128,128]{3,2,1,0:T(8,128)}), f32[8,4,128,128]{3,2,1,0:T(8,128)}) %all-gather.9.cloned.1.call-update) | async-done | bytes 2097168 | tf_op jit(solution)/shard_map/all_gather | solution.py:52
  170.5 2.6 %multiply_reduce_fusion = (f32[128,4,4]{0,2,1:T(4,128)S(1)}, f32[128,4,4,128]{0,3,2,1:T(8,128)S(1)}) fusion(bf16[128,4,4,128]{0,3,2,1:T(8,128)(2,1)S(1)} %bitcast.203, f32[8,4,128,128]{3,2,1,0:T(8,128)} %all-gather.9.cloned.1.call-done, f32[8,128,128]{2,1,0:T(8,128)S(1)} %all-gather.2, pred[]{:T(512)S(6)} %lt.43, pred[]{:T(512)S(6)} %and.43, pred[]{:T(512)S(6)} %gt.31, ...), kind=kOutput, calls=%fused_computation.31 | convolution fusion | flops 405993472 | bytes 4202654 | tf_op jit(solution)/shard_map/rgqd,gde->rgqe/dot_general | solution.py:203
  173.6 1.3 copy.52
  (90 shorter events, 8.4 us)
Async XLA Ops:
  6.5 5.3 %copy-start.2 = (s32[128]{0:T(128)S(1)}, s32[128]{0:T(128)}, u32[]{:S(2)}) copy-start(s32[128]{0:T(128)} %param.13) | copy-start | bytes 1540
  6.5 52.2 %all-gather.7.cloned.1.call-start = ((), (), s32[]{:S(2)}) async-start(), calls=%async_computation | async-start | bytes 2359296 | tf_op jit(solution)/shard_map/all_gather | solution.py:17
  8.3 162.2 %all-gather.9.cloned.1.call-start = ((), (), s32[]{:S(2)}) async-start(), calls=%async_computation.1 | async-start | bytes 2359296 | tf_op jit(solution)/shard_map/all_gather | solution.py:52
  9.7 51.8 %copy-start = (bf16[128,2048]{0,1:T(8,128)(2,1)}, bf16[128,2048]{0,1:T(8,128)(2,1)S(1)}, u32[]{:S(2)}) copy-start(bf16[128,2048]{0,1:T(8,128)(2,1)S(1)} %copy.45) | copy-start | bytes 1572868
  61.5 60.2 %copy-start.4 = (f32[16]{0:T(128)S(1)}, f32[16]{0:T(128)}, u32[]{:S(2)}) copy-start(f32[16]{0:T(128)} %param.14) | copy-start | bytes 196
  110.5 60.0 %copy-start.1 = (bf16[128,2048]{0,1:T(8,128)(2,1)S(1)}, bf16[128,2048]{0,1:T(8,128)(2,1)}, u32[]{:S(2)}) copy-start(bf16[128,2048]{0,1:T(8,128)(2,1)} %copy-done) | copy-start | bytes 1572868
  161.3 11.8 %copy-start.3 = (f32[2048]{0:T(1024)S(1)}, f32[2048]{0:T(1024)}, u32[]{:S(2)}) copy-start(f32[2048]{0:T(1024)} %param.15) | copy-start | bytes 24580
Sparse Core Ops, SparseCore 0:
  9.4 49.2 all-gather.6
  120.1 50.3 all-gather.8
where the time goes:
time: 183 us; the launch traced here: 182 us
  between operations  43.2 us (24%)
  blocking collectives  39.9 us (22%)
  waiting for transfers between devices  33.8 us (18%)
  local copies, waits for them, and re-layouts  29.4 us (16%)
  loops' own time  21.2 us (12%)
  other arithmetic  8.77 us (5%)
  matrix products  5.49 us (3%)
    all_gather x1, waiting for transfers between devices, in_one_piece(): out = lax.all_gather(both, axis, axis=dim, tiled=True)  24.7 us
    all_gather x1, blocking collectives, on_device(): lax.all_gather(doc_ids, 'kv', axis=0, tiled=True)  22.2 us
    another operation x1, loops' own time, on_device(): result, _ = lax.scan(one_block, (initial, empty_tail), stacked)  21 us
    unnamed x2, blocking collectives  15.3 us
    dynamic_slice x40, local copies, waits for them, and re-layouts, on_device(): result, _ = lax.scan(one_block, (initial, empty_tail), stacked)  14.4 us
    all_gather x1, waiting for transfers between devices, collected_alike(): lax.all_gather(a, axis)  9.14 us
    eq x8, other arithmetic, tail_state(): live = doc_rows == target_doc  5.13 us
    slice x8, local copies, waits for them, and re-layouts, one_block(): doc_block[0]  4.86 us
  transfers between devices with their start and end apart: 2, of which 2 were waited for; matrix products, arithmetic and copies ran while one was open for 3% of the time, Pallas kernels for 0%

commit v1 on v0

v1 whole, which is shorter than its diff:
```python
import functools
import math

import jax
import jax.numpy as jnp
from jax import lax
from jax.experimental import pallas as pl
from jax.experimental.pallas import tpu as pltpu
from jax.sharding import PartitionSpec as P

HEADS = 16
GROUPS = 4
D = 128
MESH = pl.DeviceIdType.MESH
F32 = jnp.float32
BF16 = jnp.bfloat16
HOPS = (4, 3, 3, 4)


def kernel(n_kv, n_seq, rows, q_hbm, k_hbm, v_hbm, docs_ref, beta_ref, gain_ref, out_hbm,
           q_vm, k_vm, kb, vb, docs, bias, tail, att, t_own, t_oth, c_own, c_in,
           in_sem, out_sem, ring_send, ring_recv, doc_send, doc_recv, st_send, st_recv):
    me = lax.axis_index("kv")
    seq = lax.axis_index("seq")
    right, left = lax.rem(me + 1, n_kv), lax.rem(me + n_kv - 1, n_kv)
    core = lax.rem(seq, 2)
    other = seq + 1 - 2 * core
    chip = seq // 2

    def along(step):
        return lax.rem(seq + 2 * step + n_seq, n_seq)

    def k_in(g):
        return pltpu.make_async_copy(k_hbm.at[:, pl.ds(g * D, D)], k_vm.at[g], in_sem.at[g])

    def v_in(g):
        return pltpu.make_async_copy(v_hbm.at[:, pl.ds(g * D, D)], vb.at[g, me], in_sem.at[GROUPS + g])

    def q_in(h):
        cols = pl.ds(pl.multiple_of(h * D, D), D)
        return pltpu.make_async_copy(q_hbm.at[:, cols], q_vm.at[h], in_sem.at[2 * GROUPS + h])

    barrier = pltpu.get_barrier_semaphore()
    for d in range(1, n_kv):
        pl.semaphore_signal(barrier, inc=1, device_id={"kv": lax.rem(me + d, n_kv)}, device_id_type=MESH)
    for s in (other, along(1), along(2), along(-1), along(-2)):
        pl.semaphore_signal(barrier, inc=1, device_id={"seq": s}, device_id_type=MESH)
    for g in range(GROUPS):
        k_in(g).start()
        v_in(g).start()

    @pl.loop(0, HEADS)
    def _(h):
        q_in(h).start()

    docs[me] = jnp.broadcast_to(docs_ref[...], (8, rows))
    for g in range(GROUPS):
        k_in(g).wait()
        kb[g, me] = k_vm[g].T
    for g in range(GROUPS):
        v_in(g).wait()
    pl.semaphore_wait(barrier, n_kv - 1 + 5)

    def doc_copy(d):
        return pltpu.make_async_remote_copy(
            src_ref=docs.at[me], dst_ref=docs.at[me],
            send_sem=doc_send.at[d - 1], recv_sem=doc_recv.at[d - 1],
            device_id={"kv": lax.rem(me + d, n_kv)}, device_id_type=MESH)

    def doc_arrival(d):
        src = lax.rem(me - d + n_kv, n_kv)
        return pltpu.make_async_remote_copy(
            src_ref=docs.at[src], dst_ref=docs.at[src],
            send_sem=doc_send.at[d - 1], recv_sem=doc_recv.at[d - 1],
            device_id={"kv": lax.rem(me + d, n_kv)}, device_id_type=MESH)

    def ring(t, g, h):
        buf = kb if t < 2 else vb
        onward = t % 2 == 0
        blk = lax.rem(me - h + n_kv, n_kv) if onward else lax.rem(me + h, n_kv)
        return pltpu.make_async_remote_copy(
            src_ref=buf.at[g, blk], dst_ref=buf.at[g, blk],
            send_sem=ring_send.at[t, g, h], recv_sem=ring_recv.at[t, g, h],
            device_id={"kv": right if onward else left}, device_id_type=MESH)

    def arrival(t, g, h):
        buf = kb if t < 2 else vb
        onward = t % 2 == 0
        blk = lax.rem(me - h - 1 + n_kv, n_kv) if onward else lax.rem(me + h + 1, n_kv)
        return pltpu.make_async_remote_copy(
            src_ref=buf.at[g, blk], dst_ref=buf.at[g, blk],
            send_sem=ring_send.at[t, g, h], recv_sem=ring_recv.at[t, g, h],
            device_id={"kv": right if onward else left}, device_id_type=MESH)

    def first_sends(g):
        for t in range(4):
            ring(t, g, 0).start()

    def hop(g, h):
        for t in range(4):
            if h < HOPS[t]:
                arrival(t, g, h).wait_recv()
                if h + 1 < HOPS[t]:
                    ring(t, g, h + 1).start()

    def state_to_other(g):
        return pltpu.make_async_remote_copy(
            src_ref=t_own.at[g], dst_ref=t_oth.at[g],
            send_sem=st_send.at[0, g], recv_sem=st_recv.at[0, g],
            device_id={"seq": other}, device_id_type=MESH)

    def state_along(g, step):
        return pltpu.make_async_remote_copy(
            src_ref=c_own.at[g], dst_ref=c_in.at[step - 1, g],
            send_sem=st_send.at[step, g], recv_sem=st_recv.at[step, g],
            device_id={"seq": along(step)}, device_id_type=MESH)

    first_sends(0)
    for d in range(1, n_kv):
        doc_copy(d).start()
    for d in range(1, n_kv):
        doc_arrival(d).wait_recv()

    own_doc = jnp.broadcast_to(docs_ref[...].astype(F32), (rows, rows)).T
    row = lax.broadcasted_iota(jnp.int32, (rows, rows), 0)
    lane = lax.broadcasted_iota(jnp.int32, (rows, rows), 1)
    last_doc = jnp.max(docs[n_kv - 1].astype(F32), axis=1, keepdims=True)[0:1]
    first_doc = jnp.min(docs[0].astype(F32), axis=1, keepdims=True)[0:1]
    for j in range(n_kv):
        doc_j = docs[j, 0:1].astype(F32)
        allowed = (doc_j == own_doc) & (j * rows + lane <= me * rows + row)
        bias[:, j * rows:(j + 1) * rows] = jnp.where(allowed, 0.0, -1e30)
        tail[:, j * rows:(j + 1) * rows] = jnp.broadcast_to(
            jnp.where(doc_j == last_doc, 1.0, 0.0), (8, rows))
    live = jnp.where(own_doc[:, 0:1] == first_doc, 1.0, 0.0)

    @pl.loop(0, HEADS)
    def _(h):
        q_in(h).wait()

    scale = math.log2(math.e) / math.sqrt(D)

    def mixing(h):
        return jax.nn.sigmoid(jnp.full((1, D), beta_ref[h], F32))

    def attend(g, pair):
        h0 = 4 * g + 2 * pair
        q2 = jnp.concatenate([q_vm[h0], q_vm[h0 + 1]], axis=0)
        kt = jnp.concatenate([kb[g, j] for j in range(n_kv)], axis=1)
        s = jnp.dot(q2, kt, preferred_element_type=F32)
        b = bias[...]
        s = s + jnp.concatenate([b, b], axis=0)
        m = jnp.max(s, axis=-1, keepdims=True)
        p = jnp.exp2((s - m) * scale)
        total = jnp.sum(p, axis=-1, keepdims=True)
        o = jnp.dot(p.astype(BF16), vb[g].reshape(n_kv * rows, D), preferred_element_type=F32)
        o = o / total
        att[h0] = o[:rows] * (1.0 - mixing(h0))
        att[h0 + 1] = o[rows:] * (1.0 - mixing(h0 + 1))

    def tail_state(g):
        kt = jnp.concatenate([kb[g, j] for j in range(n_kv)], axis=1)
        kt = kt * tail[0:1].astype(BF16)
        t = jnp.dot(kt, vb[g].reshape(n_kv * rows, D), preferred_element_type=F32)
        t_own[g, 0:D] = t
        t_own[g, D:D + 8] = jnp.broadcast_to(last_doc, (8, D))

    def chip_state(g):
        own, oth = t_own[g], t_oth[g]
        even = jnp.where(core == 0, own, oth)
        odd = jnp.where(core == 0, oth, own)
        same = even[D:D + 1] == odd[D:D + 1]
        c_own[g, 0:D] = odd[0:D] + jnp.where(same, even[0:D], 0.0)
        c_own[g, D:D + 8] = odd[D:D + 8]

    def recall(g):
        one, two, near = c_in[0, g], c_in[1, g], t_oth[g]
        mem = jnp.where((one[D:D + 1] == first_doc) & (chip >= 1), one[0:D], 0.0)
        mem = mem + jnp.where((two[D:D + 1] == first_doc) & (chip >= 2), two[0:D], 0.0)
        mem = mem + jnp.where((near[D:D + 1] == first_doc) & (core == 1), near[0:D], 0.0)
        hi = mem.astype(BF16)
        lo = (mem - hi.astype(F32)).astype(BF16)
        both = jnp.concatenate([hi, lo], axis=1)
        q4 = jnp.concatenate([q_vm[4 * g + k] for k in range(4)], axis=0)
        r = jnp.dot(q4, both, preferred_element_type=F32)
        r = r[:, 0:D] + r[:, D:]
        for k in range(4):
            h = 4 * g + k
            rh = r[k * rows:(k + 1) * rows] * live
            mean = jnp.mean(rh * rh, axis=-1, keepdims=True)
            cols = pl.ds(pl.multiple_of(h * D, D), D)
            att[h] = att[h] + rh * lax.rsqrt(mean + 1e-6) * (gain_ref[:, cols] * mixing(h))

    def out_copy(h):
        cols = pl.ds(pl.multiple_of(h * D, D), D)
        return pltpu.make_async_copy(att.at[h], out_hbm.at[:, cols], out_sem.at[h])

    @pl.loop(0, GROUPS + 2)
    def _(n):
        @pl.when(n + 1 < GROUPS)
        def _():
            first_sends(n + 1)

        @pl.when(n >= 2)
        def _():
            g = n - 2
            state_to_other(g).wait_recv()
            chip_state(g)
            state_along(g, 1).start()
            state_along(g, 2).start()

        for half in range(2):
            @pl.when((n >= 1) & (n <= GROUPS))
            def _():
                hop(n - 1, 2 + half)

            @pl.when(n < GROUPS)
            def _():
                hop(n, half)

            if half == 1:
                @pl.when((n >= 1) & (n <= GROUPS))
                def _():
                    tail_state(n - 1)
                    state_to_other(n - 1).start()

            @pl.when(n >= 2)
            def _():
                attend(n - 2, half)

        @pl.when(n >= 2)
        def _():
            g = n - 2
            state_along(g, 1).wait_recv()
            state_along(g, 2).wait_recv()
            recall(g)
            for k in range(4):
                out_copy(4 * g + k).start()

    for d in range(1, n_kv):
        doc_copy(d).wait_send()

    @pl.loop(0, GROUPS)
    def _(g):
        for t in range(4):
            for h in range(HOPS[t]):
                ring(t, g, h).wait_send()
        state_to_other(g).wait_send()
        state_along(g, 1).wait_send()
        state_along(g, 2).wait_send()

    @pl.loop(0, HEADS)
    def _(h):
        out_copy(h).wait()


def on_device(n_kv, n_seq, queries, keys, values, doc_ids, beta, lin_gain):
    rows = queries.shape[0]
    hbm = pl.BlockSpec(memory_space=pl.ANY)
    vmem = pl.BlockSpec(memory_space=pltpu.VMEM)
    smem = pl.BlockSpec(memory_space=pltpu.SMEM)
    dma = pltpu.SemaphoreType.DMA
    return pl.pallas_call(
        functools.partial(kernel, n_kv, n_seq, rows),
        out_shape=jax.ShapeDtypeStruct((rows, HEADS * D), F32),
        in_specs=[hbm, hbm, hbm, vmem, smem, vmem],
        out_specs=hbm,
        scratch_shapes=[
            pltpu.VMEM((HEADS, rows, D), BF16),
            pltpu.VMEM((GROUPS, rows, D), BF16),
            pltpu.VMEM((GROUPS, n_kv, D, rows), BF16),
            pltpu.VMEM((GROUPS, n_kv, rows, D), BF16),
            pltpu.VMEM((n_kv, 8, rows), jnp.int32),
            pltpu.VMEM((rows, n_kv * rows), F32),
            pltpu.VMEM((8, n_kv * rows), F32),
            pltpu.VMEM((HEADS, rows, D), F32),
            pltpu.VMEM((GROUPS, D + 8, D), F32),
            pltpu.VMEM((GROUPS, D + 8, D), F32),
            pltpu.VMEM((GROUPS, D + 8, D), F32),
            pltpu.VMEM((2, GROUPS, D + 8, D), F32),
            dma((2 * GROUPS + HEADS,)),
            dma((HEADS,)),
            dma((4, GROUPS, 4)),
            dma((4, GROUPS, 4)),
            dma((n_kv - 1,)),
            dma((n_kv - 1,)),
            dma((3, GROUPS)),
            dma((3, GROUPS)),
        ],
        compiler_params=pltpu.CompilerParams(
            collective_id=0, has_side_effects=True, vmem_limit_bytes=32 * 1024 * 1024),
    )(queries, keys, values, doc_ids.reshape(1, rows), beta, lin_gain.reshape(1, HEADS * D))


def solution(mesh):
    split = P(("dp", "seq", "kv"))
    rows = P(("dp", "seq", "kv"), None)
    return jax.shard_map(
        functools.partial(on_device, mesh.shape["kv"], mesh.shape["seq"]),
        mesh=mesh, in_specs=(rows, rows, rows, split, P(), P()), out_specs=rows, check_vma=False)
```

time: 183 us -> 73.5 us (0.40)
  the two profiles are of different devices: /device:TPU:2 before, /device:TPU:1 now
where the time goes in v1:
time: 73.5 us; the launch traced here: 73.3 us
  Pallas kernels  68.1 us (93%)
  local copies, waits for them, and re-layouts  5.19 us (7%)
    pallas_call x1, Pallas kernels, on_device(): pl.pallas_call(functools.partial(kernel, n_kv, n_seq, rows), out_shape=ja...  68.1 us
    unnamed x13, local copies, waits for them, and re-layouts  5.19 us

profile of v1, /device:TPU:1, one launch (start us, length us, event | category | flops | bytes accessed | tf_op | source)
XLA Modules:
  0.0 73.3 jit_solution(1467643193573978818)
XLA Ops:
  0.0 0.0 copy-start.4
  0.0 0.0 copy-start.5
  0.0 0.7 copy-done.4
  0.7 0.0 copy-done.5
  0.7 0.0 copy-start
  0.7 1.0 %copy-done = bf16[128,2048]{1,0:T(8,128)(2,1)S(1)} copy-done((bf16[128,2048]{1,0:T(8,128)(2,1)S(1)}, bf16[128,2048]{1,0:T(8,128)(2,1)}, u32[]{:S(2)}) %copy-start) | copy-done | bytes 524312
  1.7 0.0 copy-start.1
  1.7 0.9 %copy-done.1 = bf16[128,512]{1,0:T(8,128)(2,1)S(1)} copy-done((bf16[128,512]{1,0:T(8,128)(2,1)S(1)}, bf16[128,512]{1,0:T(8,128)(2,1)}, u32[]{:S(2)}) %copy-start.1) | copy-done | bytes 131096
  2.6 0.0 copy-start.2
  2.6 0.9 %copy-done.2 = bf16[128,512]{1,0:T(8,128)(2,1)S(1)} copy-done((bf16[128,512]{1,0:T(8,128)(2,1)S(1)}, bf16[128,512]{1,0:T(8,128)(2,1)}, u32[]{:S(2)}) %copy-start.2) | copy-done | bytes 131096
  3.5 0.0 copy-start.3
  3.5 0.7 copy-done.3
  4.2 68.1 %shard_map.64 = f32[128,2048]{1,0:T(8,128)S(1)} custom-call(bf16[128,2048]{1,0:T(8,128)(2,1)S(1)} %copy-done, bf16[128,512]{1,0:T(8,128)(2,1)S(1)} %copy-done.1, bf16[128,512]{1,0:T(8,128)(2,1)S(1)} %copy-done.2, s32[1,128]{1,0:T(1,128)S(1)} %bitcast.3, f32[16]{0:T(128)S(1)} %copy-done.5, f32[1,2048]{1,0:T(1,128)S(1)} %bitcast.2), custom_call_target="tpu_custom_call" | custom-call | tf_op jit(solution)/shard_map/pallas_call | solution.py:263
  72.3 1.0 %copy.8 = f32[128,2048]{1,0:T(8,128)} copy(f32[128,2048]{1,0:T(8,128)S(1)} %shard_map.64) | data formatting | bytes 2097152
Async XLA Ops:
  0.0 0.7 copy-start.4
  0.0 0.7 copy-start.5
  0.7 1.0 %copy-start = (bf16[128,2048]{1,0:T(8,128)(2,1)S(1)}, bf16[128,2048]{1,0:T(8,128)(2,1)}, u32[]{:S(2)}) copy-start(bf16[128,2048]{1,0:T(8,128)(2,1)} %q_hbm.1) | copy-start | bytes 1572868
  1.7 0.9 %copy-start.1 = (bf16[128,512]{1,0:T(8,128)(2,1)S(1)}, bf16[128,512]{1,0:T(8,128)(2,1)}, u32[]{:S(2)}) copy-start(bf16[128,512]{1,0:T(8,128)(2,1)} %k_hbm.1) | copy-start | bytes 393220
  2.6 0.9 %copy-start.2 = (bf16[128,512]{1,0:T(8,128)(2,1)S(1)}, bf16[128,512]{1,0:T(8,128)(2,1)}, u32[]{:S(2)}) copy-start(bf16[128,512]{1,0:T(8,128)(2,1)} %v_hbm.1) | copy-start | bytes 393220
  3.5 0.7 copy-start.3

commit v2 on v1

v2 whole, which is shorter than its diff:
```python
import functools
import math

import jax
import jax.numpy as jnp
from jax import lax
from jax.experimental import pallas as pl
from jax.experimental.pallas import tpu as pltpu
from jax.sharding import PartitionSpec as P

HEADS = 16
GROUPS = 4
D = 128
MESH = pl.DeviceIdType.MESH
F32 = jnp.float32
BF16 = jnp.bfloat16
NEG = -1e30
NEAR = (-2, -1, 0, 1, 2)
FAR = (-3, 3, 4)


def kernel(n_kv, n_seq, rows, q_hbm, k_hbm, v_hbm, docs_ref, beta_ref, gain_ref, out_hbm,
           q_vm, k_vm, kv, docs, bias, top, total, acc, att, p_own, p_in, t_own, t_oth, c_own, c_in, x_own, x_in, mem,
           in_sem, out_sem, ring_send, ring_recv, doc_send, doc_recv, p_send, p_recv, st_send, st_recv, mem_send, mem_recv):
    me = lax.axis_index("kv")
    seq = lax.axis_index("seq")
    core = lax.rem(seq, 2)
    other = seq + 1 - 2 * core
    chip = seq // 2
    half = n_kv // 2
    mine = lax.rem(me, GROUPS)

    def away(step):
        return lax.rem(me + step + n_kv, n_kv)

    def along(step):
        return lax.rem(seq + 2 * step + n_seq, n_seq)

    odd_step = 4 * lax.rem(me, 2) - 2
    barrier = pltpu.get_barrier_semaphore()
    for d in range(1, n_kv):
        pl.semaphore_signal(barrier, inc=1, device_id={"kv": away(d)}, device_id_type=MESH)
    for d in (other, along(1), along(2), along(-1), along(-2)):
        pl.semaphore_signal(barrier, inc=1, device_id={"seq": d}, device_id_type=MESH)

    def k_in(g):
        return pltpu.make_async_copy(k_hbm.at[:, pl.ds(g * D, D)], k_vm.at[g], in_sem.at[g])

    def v_in(g):
        return pltpu.make_async_copy(
            v_hbm.at[:, pl.ds(g * D, D)], kv.at[g, me, pl.ds(D, rows)], in_sem.at[GROUPS + g])

    def q_in(h):
        cols = pl.ds(pl.multiple_of(h * D, D), D)
        return pltpu.make_async_copy(q_hbm.at[:, cols], q_vm.at[h], in_sem.at[2 * GROUPS + h])

    for g in range(GROUPS):
        k_in(g).start()
    for g in range(GROUPS):
        v_in(g).start()
    for h in range(HEADS):
        q_in(h).start()
    docs[me] = jnp.broadcast_to(docs_ref[...].astype(BF16), (16, rows))
    for j in range(half, n_kv):
        @pl.when(j > me)
        def _():
            for g in range(GROUPS):
                kv[g, j] = jnp.zeros((D + rows, D), BF16)
    for g in range(GROUPS):
        k_in(g).wait()
        kv[g, me, 0:D] = k_vm[g].T
    own_row = docs_ref[...].astype(F32)
    ending = jnp.where(own_row == jnp.max(own_row, axis=1, keepdims=True), 1.0, 0.0).astype(BF16)
    for g in range(GROUPS):
        v_in(g).wait()
        p_own[g] = jnp.dot(kv[g, me, 0:D] * ending, kv[g, me, D:D + rows], preferred_element_type=F32)
    pl.semaphore_wait(barrier, n_kv - 1 + 5)

    def doc_copy(d, ahead):
        blk = away(-d) if ahead else me
        return pltpu.make_async_remote_copy(
            src_ref=docs.at[blk], dst_ref=docs.at[blk],
            send_sem=doc_send.at[d - 1], recv_sem=doc_recv.at[d - 1],
            device_id={"kv": away(d)}, device_id_type=MESH)

    def part_copy(slot):
        step = (1, -1, odd_step)[slot]
        g = lax.rem(me + (1, GROUPS - 1, 2)[slot], GROUPS)
        return pltpu.make_async_remote_copy(
            src_ref=p_own.at[g], dst_ref=p_in.at[slot],
            send_sem=p_send.at[slot], recv_sem=p_recv.at[slot],
            device_id={"kv": away(step)}, device_id_type=MESH)

    def span(h, onward):
        if h < half - 1:
            return pl.ds(0, D + rows)
        return pl.ds(0, D) if onward else pl.ds(D, rows)

    def ring(onward, g, h, ahead):
        blk = away(-h - ahead if onward else h + ahead)
        ref = kv.at[g, blk, span(h, onward)]
        t = 0 if onward else 1
        return pltpu.make_async_remote_copy(
            src_ref=ref, dst_ref=ref, send_sem=ring_send.at[t, g, h], recv_sem=ring_recv.at[t, g, h],
            device_id={"kv": away(1 if onward else -1)}, device_id_type=MESH)

    def sent(h, onward):
        return (me >= h) & (me < n_kv - 1) if onward else away(h) < half

    def arrives(h, onward):
        return me > h if onward else away(h + 1) < half

    def send(g, h):
        for onward in (True, False):
            @pl.when(sent(h, onward))
            def _():
                ring(onward, g, h, 0).start()

    def hop(g, h):
        for onward in (True, False):
            @pl.when(arrives(h, onward))
            def _():
                ring(onward, g, h, 1).wait_recv()
            if h + 1 < half:
                @pl.when(sent(h + 1, onward))
                def _():
                    ring(onward, g, h + 1, 0).start()

    def state_to_other():
        return pltpu.make_async_remote_copy(
            src_ref=t_own, dst_ref=t_oth, send_sem=st_send.at[0], recv_sem=st_recv.at[0],
            device_id={"seq": other}, device_id_type=MESH)

    def state_along(step):
        return pltpu.make_async_remote_copy(
            src_ref=c_own, dst_ref=c_in.at[step - 1], send_sem=st_send.at[step], recv_sem=st_recv.at[step],
            device_id={"seq": along(step)}, device_id_type=MESH)

    def state_across():
        return pltpu.make_async_remote_copy(
            src_ref=x_own, dst_ref=x_in, send_sem=st_send.at[3], recv_sem=st_recv.at[3],
            device_id={"kv": away(half)}, device_id_type=MESH)

    def memory_out(slot):
        target = away((1, -1, odd_step)[slot])
        return pltpu.make_async_remote_copy(
            src_ref=mem.at[mine], dst_ref=mem.at[mine],
            send_sem=mem_send.at[slot], recv_sem=mem_recv.at[slot],
            device_id={"kv": target}, device_id_type=MESH)

    def memory_in(slot):
        g = lax.rem(me + (GROUPS - 1, 1, 2)[slot], GROUPS)
        return pltpu.make_async_remote_copy(
            src_ref=mem.at[g], dst_ref=mem.at[g],
            send_sem=mem_send.at[slot], recv_sem=mem_recv.at[slot],
            device_id={"kv": away(1)}, device_id_type=MESH)

    own_doc = jnp.broadcast_to(docs_ref[...].astype(F32), (rows, rows)).T

    def doc_row(j):
        return docs[j].astype(F32)[0:1]

    def ends():
        last = jnp.max(doc_row(n_kv - 1), axis=1, keepdims=True)
        first = jnp.min(doc_row(0), axis=1, keepdims=True)
        return first, last

    def masks():
        row = lax.broadcasted_iota(jnp.int32, (rows, rows), 0)
        lane = lax.broadcasted_iota(jnp.int32, (rows, rows), 1)
        for j in range(n_kv):
            allowed = (doc_row(j) == own_doc) & (j * rows + lane <= me * rows + row)
            bias[j] = jnp.where(allowed, 0.0, NEG)

    scale = math.log2(math.e) / math.sqrt(D)

    def mixing(h):
        return jax.nn.sigmoid(jnp.full((1, D), beta_ref[h], F32))

    def scores(i, offs):
        g = i // 2
        q2 = jnp.concatenate([q_vm[2 * i], q_vm[2 * i + 1]], axis=0)
        kt = jnp.concatenate([kv[g, away(o), 0:D] for o in offs], axis=1)
        b = jnp.concatenate([bias[away(o)] for o in offs], axis=1)
        s = jnp.dot(q2, kt, preferred_element_type=F32)
        return s + jnp.concatenate([b, b], axis=0)

    def weighted(i, offs, p):
        v = jnp.concatenate([kv[i // 2, away(o), D:D + rows] for o in offs], axis=0)
        return jnp.dot(p.astype(BF16), v, preferred_element_type=F32)

    def near(i):
        s = scores(i, NEAR)
        m = jnp.max(s, axis=-1, keepdims=True)
        p = jnp.exp2((s - m) * scale)
        top[i] = m
        total[i] = jnp.sum(p, axis=-1, keepdims=True)
        acc[i] = weighted(i, NEAR, p)

    def far(i):
        s = scores(i, FAR)
        old = top[i]
        m = jnp.maximum(old, jnp.max(s, axis=-1, keepdims=True))
        p = jnp.exp2((s - m) * scale)
        kept = jnp.exp2((old - m) * scale)
        norm = total[i] * kept + jnp.sum(p, axis=-1, keepdims=True)
        o = (acc[i] * kept + weighted(i, FAR, p)) / norm
        att[2 * i] = o[:rows] * (1.0 - mixing(2 * i))
        att[2 * i + 1] = o[rows:] * (1.0 - mixing(2 * i + 1))

    def some(f, start, stop):
        pl.loop(start, stop)(f)

    def tail_state():
        for slot in range(3):
            part_copy(slot).wait_recv()
        last_doc = ends()[1]

        def counted(blk, part):
            here = jnp.max(doc_row(blk), axis=1, keepdims=True)
            return jnp.where(here == last_doc, part, 0.0)

        t_own[0:D] = (counted(me, p_own[mine]) + counted(away(-1), p_in[0])
                      + counted(away(1), p_in[1]) + counted(away(-odd_step), p_in[2]))
        t_own[D:D + 8] = jnp.broadcast_to(last_doc, (8, D))
        state_to_other().start()

    def chip_state():
        state_to_other().wait_recv()
        own, oth = t_own[...], t_oth[...]
        even = jnp.where(core == 0, own, oth)
        odd = jnp.where(core == 0, oth, own)
        same = even[D:D + 1] == odd[D:D + 1]
        c_own[0:D] = odd[0:D] + jnp.where(same, even[0:D], 0.0)
        c_own[D:D + 8] = odd[D:D + 8]
        state_along(1).start()
        state_along(2).start()

    def part_memory():
        first_doc = ends()[0]
        state_along(1).wait_recv()
        state_along(2).wait_recv()
        one, two, beside = c_in[0], c_in[1], t_oth[...]
        part = jnp.where((one[D:D + 1] == first_doc) & (chip >= 1), one[0:D], 0.0)
        part = part + jnp.where((two[D:D + 1] == first_doc) & (chip >= 2), two[0:D], 0.0)
        part = part + jnp.where((beside[D:D + 1] == first_doc) & (core == 1), beside[0:D], 0.0)
        x_own[...] = part
        state_across().start()

    def own_memory():
        state_across().wait_recv()
        mem[mine] = x_own[...] + x_in[...]
        for slot in range(3):
            memory_out(slot).start()

    def out_copy(h):
        cols = pl.ds(pl.multiple_of(h * D, D), D)
        return pltpu.make_async_copy(att.at[h], out_hbm.at[:, cols], out_sem.at[h])

    def recall(g):
        live = jnp.where(own_doc[:, 0:1] == ends()[0], 1.0, 0.0)
        state = mem[g]
        hi = state.astype(BF16)
        lo = (state - hi.astype(F32)).astype(BF16)
        both = jnp.concatenate([hi, lo], axis=1)
        q4 = jnp.concatenate([q_vm[4 * g + k] for k in range(4)], axis=0)
        r = jnp.dot(q4, both, preferred_element_type=F32)
        r = r[:, 0:D] + r[:, D:]
        for k in range(4):
            h = 4 * g + k
            rh = r[k * rows:(k + 1) * rows] * live
            mean = jnp.mean(rh * rh, axis=-1, keepdims=True)
            cols = pl.ds(pl.multiple_of(h * D, D), D)
            att[h] = att[h] + rh * lax.rsqrt(mean + 1e-6) * (gain_ref[:, cols] * mixing(h))
            out_copy(h).start()

    for d in range(1, n_kv):
        doc_copy(d, False).start()
    for slot in range(3):
        part_copy(slot).start()
    for g in range(GROUPS):
        send(g, 0)
    for d in range(1, n_kv):
        doc_copy(d, True).wait_recv()
    masks()
    tail_state()
    hop(0, 0)
    chip_state()
    for h in range(HEADS):
        q_in(h).wait()
    hop(1, 0)
    hop(2, 0)
    hop(3, 0)
    hop(0, 1)
    hop(1, 1)
    part_memory()
    some(near, 0, 1)
    hop(2, 1)
    some(near, 1, 3)
    hop(3, 1)
    some(near, 3, 4)
    hop(0, 2)
    some(near, 4, 5)
    own_memory()
    hop(1, 2)
    some(near, 5, 6)
    hop(2, 2)
    some(near, 6, 7)
    hop(3, 2)
    some(near, 7, 8)
    for slot in range(3):
        memory_in(slot).wait_recv()
    hop(0, 3)
    some(far, 0, 2)
    some(recall, 0, 1)
    hop(1, 3)
    some(far, 2, 4)
    some(recall, 1, 2)
    hop(2, 3)
    some(far, 4, 6)
    some(recall, 2, 3)
    hop(3, 3)
    some(far, 6, 8)
    some(recall, 3, 4)

    for h in range(half):
        for onward in (True, False):
            @pl.when(sent(h, onward))
            def _():
                for g in range(GROUPS):
                    ring(onward, g, h, 0).wait_send()
    for d in range(1, n_kv):
        doc_copy(d, False).wait_send()
    for slot in range(3):
        part_copy(slot).wait_send()
    state_to_other().wait_send()
    state_along(1).wait_send()
    state_along(2).wait_send()
    state_across().wait_send()
    for slot in range(3):
        memory_out(slot).wait_send()
    for h in range(HEADS):
        out_copy(h).wait()


def on_device(n_kv, n_seq, queries, keys, values, doc_ids, beta, lin_gain):
    rows = queries.shape[0]
    hbm = pl.BlockSpec(memory_space=pl.ANY)
    vmem = pl.BlockSpec(memory_space=pltpu.VMEM)
    smem = pl.BlockSpec(memory_space=pltpu.SMEM)
    dma = pltpu.SemaphoreType.DMA
    state = pltpu.VMEM((D + 8, D), F32)
    return pl.pallas_call(
        functools.partial(kernel, n_kv, n_seq, rows),
        out_shape=jax.ShapeDtypeStruct((rows, HEADS * D), F32),
        in_specs=[hbm, hbm, hbm, vmem, smem, vmem],
        out_specs=hbm,
        scratch_shapes=[
            pltpu.VMEM((HEADS, rows, D), BF16),
            pltpu.VMEM((GROUPS, rows, D), BF16),
            pltpu.VMEM((GROUPS, n_kv, D + rows, D), BF16),
            pltpu.VMEM((n_kv, 16, rows), BF16),
            pltpu.VMEM((n_kv, rows, rows), F32),
            pltpu.VMEM((HEADS // 2, 2 * rows, 1), F32),
            pltpu.VMEM((HEADS // 2, 2 * rows, 1), F32),
            pltpu.VMEM((HEADS // 2, 2 * rows, D), F32),
            pltpu.VMEM((HEADS, rows, D), F32),
            pltpu.VMEM((GROUPS, D, D), F32),
            pltpu.VMEM((3, D, D), F32),
            state, state, state,
            pltpu.VMEM((2, D + 8, D), F32),
            pltpu.VMEM((D, D), F32),
            pltpu.VMEM((D, D), F32),
            pltpu.VMEM((GROUPS, D, D), F32),
            dma((2 * GROUPS + HEADS,)),
            dma((HEADS,)),
            dma((2, GROUPS, n_kv // 2)),
            dma((2, GROUPS, n_kv // 2)),
            dma((n_kv - 1,)),
            dma((n_kv - 1,)),
            dma((3,)),
            dma((3,)),
            dma((4,)),
            dma((4,)),
            dma((3,)),
            dma((3,)),
        ],
        compiler_params=pltpu.CompilerParams(
            collective_id=0, has_side_effects=True, vmem_limit_bytes=60 * 1024 * 1024),
    )(queries, keys, values, doc_ids.reshape(1, rows), beta, lin_gain.reshape(1, HEADS * D))


def solution(mesh):
    split = P(("dp", "seq", "kv"))
    rows = P(("dp", "seq", "kv"), None)
    return jax.shard_map(
        functools.partial(on_device, mesh.shape["kv"], mesh.shape["seq"]),
        mesh=mesh, in_specs=(rows, rows, rows, split, P(), P()), out_specs=rows, check_vma=False)
```

time: 73.5 us -> 52.1 us (0.71)
  the two profiles are of different devices: /device:TPU:1 before, /device:TPU:4 now
where the time goes in v2:
time: 52.1 us; the launch traced here: 51.8 us
  Pallas kernels  49.5 us (95%)
  local copies, waits for them, and re-layouts  2.3 us (4%)
    pallas_call x1, Pallas kernels, on_device(): pl.pallas_call(functools.partial(kernel, n_kv, n_seq, rows), out_shape=ja...  49.5 us
    unnamed x1, local copies, waits for them, and re-layouts  2.3 us

profile of v2, /device:TPU:4, one launch (start us, length us, event | category | flops | bytes accessed | tf_op | source)
XLA Modules:
  0.0 51.8 jit_solution(6850399250930010763)
XLA Ops:
  0.0 49.5 %shard_map.64 = f32[128,2048]{1,0:T(8,128)} custom-call(bf16[128,2048]{1,0:T(8,128)(2,1)} %q_hbm.1, bf16[128,512]{1,0:T(8,128)(2,1)} %k_hbm.1, bf16[128,512]{1,0:T(8,128)(2,1)} %v_hbm.1, s32[1,128]{1,0:T(1,128)} %bitcast.3, f32[16]{0:T(128)} %beta_ref.1, f32[1,2048]{1,0:T(1,128)} %bitcast.2), custom_call_target="tpu_custom_call" | custom-call | tf_op jit(solution)/shard_map/pallas_call | solution.py:353
  49.5 2.3 %copy.8 = f32[128,2048]{1,0:T(8,128)} copy(f32[128,2048]{1,0:T(8,128)} %shard_map.64) | data formatting | bytes 2097152

commit v3 on v2

v3 whole, which is shorter than its diff:
```python
import functools
import math

import jax
import jax.numpy as jnp
from jax import lax
from jax.experimental import pallas as pl
from jax.experimental.pallas import tpu as pltpu
from jax.sharding import PartitionSpec as P

HEADS = 16
GROUPS = 4
D = 128
MESH = pl.DeviceIdType.MESH
F32 = jnp.float32
BF16 = jnp.bfloat16
NEG = -1e30
NEAR = (-2, -1, 0, 1, 2)
FAR = (-3, 3, 4)


def kernel(n_kv, n_seq, rows, q_hbm, k_hbm, v_hbm, docs_hbm, beta_hbm, gain_hbm, out_hbm,
           docs_ref, beta_ref, gain_ref, q_vm, k_vm, kv, docs, bias, top, total, acc, att, p_own, p_in, c_own, c_in, x_own, x_in, m_own, mem,
           in_sem, out_sem, ring_send, ring_recv, doc_send, doc_recv, p_send, p_recv, st_send, st_recv, mem_send, mem_recv):
    me = lax.axis_index("kv")
    seq = lax.axis_index("seq")
    core = lax.rem(seq, 2)
    other = seq + 1 - 2 * core
    chip = seq // 2
    half = n_kv // 2
    part = D // 2
    mine = 2 * lax.rem(me, GROUPS) + core
    odd_step = 4 * lax.rem(me, 2) - 2
    steps = (1, -1, odd_step, 0)

    def away(step):
        return lax.rem(me + step + n_kv, n_kv)

    def along(step):
        return lax.rem(seq + 2 * step + n_seq, n_seq)

    barrier = pltpu.get_barrier_semaphore()
    for d in range(1, n_kv):
        pl.semaphore_signal(barrier, inc=1, device_id={"kv": away(d)}, device_id_type=MESH)
        pl.semaphore_signal(barrier, inc=1, device_id={"kv": away(d), "seq": other}, device_id_type=MESH)
    for d in (other, along(1), along(2), along(-1), along(-2)):
        pl.semaphore_signal(barrier, inc=1, device_id={"seq": d}, device_id_type=MESH)

    def k_in(g):
        return pltpu.make_async_copy(k_hbm.at[:, pl.ds(g * D, D)], k_vm.at[g], in_sem.at[g])

    def v_in(g):
        return pltpu.make_async_copy(
            v_hbm.at[:, pl.ds(g * D, D)], kv.at[g, me, pl.ds(D, rows)], in_sem.at[GROUPS + g])

    def q_in(h):
        cols = pl.ds(pl.multiple_of(h * D, D), D)
        return pltpu.make_async_copy(q_hbm.at[:, cols], q_vm.at[h], in_sem.at[2 * GROUPS + h])

    smalls = [pltpu.make_async_copy(a, b, in_sem.at[2 * GROUPS + HEADS + n]) for n, (a, b) in enumerate(
        ((docs_hbm, docs_ref), (beta_hbm, beta_ref), (gain_hbm, gain_ref)))]
    smalls[0].start()
    for g in range(GROUPS):
        k_in(g).start()
    for g in range(GROUPS):
        v_in(g).start()
    smalls[1].start()
    smalls[2].start()
    for h in range(HEADS):
        q_in(h).start()
    smalls[0].wait()
    docs[core, me] = jnp.broadcast_to(docs_ref[...].astype(BF16), (16, rows))
    for j in range(half, n_kv):
        @pl.when(j > me)
        def _():
            for g in range(GROUPS):
                kv[g, j] = jnp.zeros((D + rows, D), BF16)
    for g in range(GROUPS):
        k_in(g).wait()
        kv[g, me, 0:D] = k_vm[g].T
    own_row = docs_ref[...].astype(F32)
    own_last = jnp.max(own_row, axis=1, keepdims=True)
    ending = jnp.where(own_row == own_last, 1.0, 0.0).astype(BF16)
    for g in range(GROUPS):
        v_in(g).wait()
        p = jnp.dot(kv[g, me, 0:D] * ending, kv[g, me, D:D + rows], preferred_element_type=F32)
        for n in range(D // part):
            p_own[g * (D // part) + n] = p[n * part:(n + 1) * part]
    pl.semaphore_wait(barrier, 2 * (n_kv - 1) + 5)

    def core_at(same):
        return (core, seq) if same else (1 - core, other)

    others = [(d, same) for d in range(n_kv) for same in (True, False) if d or not same]
    partners = [(n, same) for n in range(4) for same in (True, False) if n < 3 or not same]

    def doc_copy(d, same):
        c, s = core_at(same)
        ref = docs.at[core, me]
        return pltpu.make_async_remote_copy(
            src_ref=ref, dst_ref=ref, send_sem=doc_send.at[d, c], recv_sem=doc_recv.at[d, core],
            device_id={"kv": away(d), "seq": s}, device_id_type=MESH)

    def doc_arrival(d, same):
        c, s = core_at(same)
        ref = docs.at[c, away(-d)]
        return pltpu.make_async_remote_copy(
            src_ref=ref, dst_ref=ref, send_sem=doc_send.at[d, c], recv_sem=doc_recv.at[d, c],
            device_id={"kv": away(d), "seq": other}, device_id_type=MESH)

    def part_copy(n, same):
        c, s = core_at(same)
        to = away(steps[n])
        return pltpu.make_async_remote_copy(
            src_ref=p_own.at[2 * lax.rem(to, GROUPS) + c], dst_ref=p_in.at[n, core],
            send_sem=p_send.at[n, c], recv_sem=p_recv.at[n, core],
            device_id={"kv": to, "seq": s}, device_id_type=MESH)

    def part_arrival(n, same):
        c, s = core_at(same)
        return pltpu.make_async_remote_copy(
            src_ref=p_own.at[mine], dst_ref=p_in.at[n, c],
            send_sem=p_send.at[n, c], recv_sem=p_recv.at[n, c],
            device_id={"kv": me, "seq": other}, device_id_type=MESH)

    def span(h, onward):
        if h < half - 1:
            return pl.ds(0, D + rows)
        return pl.ds(0, D) if onward else pl.ds(D, rows)

    def ring(onward, g, h, ahead):
        blk = away(-h - ahead if onward else h + ahead)
        ref = kv.at[g, blk, span(h, onward)]
        t = 0 if onward else 1
        return pltpu.make_async_remote_copy(
            src_ref=ref, dst_ref=ref, send_sem=ring_send.at[t, g, h], recv_sem=ring_recv.at[t, g, h],
            device_id={"kv": away(1 if onward else -1)}, device_id_type=MESH)

    def sent(h, onward):
        return (me >= h) & (me < n_kv - 1) if onward else away(h) < half

    def arrives(h, onward):
        return me > h if onward else away(h + 1) < half

    def send(g, h):
        for onward in (True, False):
            @pl.when(sent(h, onward))
            def _():
                ring(onward, g, h, 0).start()

    def hop(g, h):
        for onward in (True, False):
            @pl.when(arrives(h, onward))
            def _():
                ring(onward, g, h, 1).wait_recv()
            if h + 1 < half:
                @pl.when(sent(h + 1, onward))
                def _():
                    ring(onward, g, h + 1, 0).start()

    def state_along(step):
        return pltpu.make_async_remote_copy(
            src_ref=c_own, dst_ref=c_in.at[step - 1], send_sem=st_send.at[step - 1], recv_sem=st_recv.at[step - 1],
            device_id={"seq": along(step)}, device_id_type=MESH)

    def state_across():
        return pltpu.make_async_remote_copy(
            src_ref=x_own, dst_ref=x_in, send_sem=st_send.at[2], recv_sem=st_recv.at[2],
            device_id={"kv": away(half)}, device_id_type=MESH)

    def memory_out(n, same):
        c, s = core_at(same)
        return pltpu.make_async_remote_copy(
            src_ref=m_own.at[c], dst_ref=mem.at[mine],
            send_sem=mem_send.at[n, c], recv_sem=mem_recv.at[n, core],
            device_id={"kv": away(steps[n]), "seq": s}, device_id_type=MESH)

    def memory_in(n, same):
        c, s = core_at(same)
        g = lax.rem(me + (GROUPS - 1, 1, 2, 0)[n], GROUPS)
        return pltpu.make_async_remote_copy(
            src_ref=m_own.at[c], dst_ref=mem.at[2 * g + c], send_sem=mem_send.at[n, c], recv_sem=mem_recv.at[n, c],
            device_id={"kv": me, "seq": other}, device_id_type=MESH)

    own_doc = jnp.broadcast_to(own_row, (rows, rows)).T

    def doc_row(j, c=None):
        return docs[core if c is None else c, j].astype(F32)[0:1]

    def ends():
        last = jnp.max(doc_row(n_kv - 1), axis=1, keepdims=True)
        first = jnp.min(doc_row(0), axis=1, keepdims=True)
        return first, last

    def masks():
        row = lax.broadcasted_iota(jnp.int32, (rows, rows), 0)
        lane = lax.broadcasted_iota(jnp.int32, (rows, rows), 1)
        for j in range(n_kv):
            allowed = (doc_row(j) == own_doc) & (j * rows + lane <= me * rows + row)
            bias[j] = jnp.where(allowed, 0.0, NEG)

    scale = math.log2(math.e) / math.sqrt(D)

    def mixing(h):
        return jax.nn.sigmoid(jnp.full((1, D), beta_ref[h], F32))

    def scores(i, offs):
        g = i // 2
        q2 = jnp.concatenate([q_vm[2 * i], q_vm[2 * i + 1]], axis=0)
        kt = jnp.concatenate([kv[g, away(o), 0:D] for o in offs], axis=1)
        b = jnp.concatenate([bias[away(o)] for o in offs], axis=1)
        s = jnp.dot(q2, kt, preferred_element_type=F32)
        return s + jnp.concatenate([b, b], axis=0)

    def weighted(i, offs, p):
        v = jnp.concatenate([kv[i // 2, away(o), D:D + rows] for o in offs], axis=0)
        return jnp.dot(p.astype(BF16), v, preferred_element_type=F32)

    def near(i):
        s = scores(i, NEAR)
        m = jnp.max(s, axis=-1, keepdims=True)
        p = jnp.exp2((s - m) * scale)
        top[i] = m
        total[i] = jnp.sum(p, axis=-1, keepdims=True)
        acc[i] = weighted(i, NEAR, p)

    def far(i):
        s = scores(i, FAR)
        old = top[i]
        m = jnp.maximum(old, jnp.max(s, axis=-1, keepdims=True))
        p = jnp.exp2((s - m) * scale)
        kept = jnp.exp2((old - m) * scale)
        norm = total[i] * kept + jnp.sum(p, axis=-1, keepdims=True)
        o = (acc[i] * kept + weighted(i, FAR, p)) / norm
        att[2 * i] = o[:rows] * (1.0 - mixing(2 * i))
        att[2 * i + 1] = o[rows:] * (1.0 - mixing(2 * i + 1))

    def settle(i):
        o = acc[i] / total[i]
        att[2 * i] = o[:rows] * (1.0 - mixing(2 * i))
        att[2 * i + 1] = o[rows:] * (1.0 - mixing(2 * i + 1))

    def rest(i):
        pl.when(me >= 3)(lambda: far(i))
        pl.when(me < 3)(lambda: settle(i))

    def some(f, start, stop):
        pl.loop(start, stop)(f)

    def edges(c):
        last = jnp.max(doc_row(n_kv - 1, c), axis=1, keepdims=True)
        first = jnp.min(doc_row(0, c), axis=1, keepdims=True)
        return first, last

    def tail_state():
        p_in[3, core] = p_own[mine]
        for n, same in partners:
            part_arrival(n, same).wait_recv()
        states = []
        for c in range(2):
            first, last = edges(c)

            def counted(n):
                here = jnp.max(doc_row(away(-steps[n]), c), axis=1, keepdims=True)
                return jnp.where(here == last, p_in[n, c], 0.0)

            states.append((sum(counted(n) for n in range(4)), first, last))
        (even, _, even_last), (odd, odd_first, odd_last) = states
        c_own[0:part] = odd + jnp.where(even_last == odd_last, even, 0.0)
        c_own[part:part + 8] = jnp.broadcast_to(odd_last, (8, D))
        state_along(1).start()
        state_along(2).start()
        x_own[1] = jnp.where(even_last == odd_first, even, 0.0)

    def part_memory():
        state_along(1).wait_recv()
        state_along(2).wait_recv()
        one, two = c_in[0], c_in[1]
        for c in range(2):
            first = edges(c)[0]
            m = jnp.where((one[part:part + 1] == first) & (chip >= 1), one[0:part], 0.0)
            m = m + jnp.where((two[part:part + 1] == first) & (chip >= 2), two[0:part], 0.0)
            x_own[c] = m + x_own[1] if c else m
        state_across().start()

    def own_memory():
        state_across().wait_recv()
        m_own[...] = x_own[...] + x_in[...]
        mem[mine] = x_own[core] + x_in[core]
        for n, same in partners:
            memory_out(n, same).start()

    def out_copy(h):
        cols = pl.ds(pl.multiple_of(h * D, D), D)
        return pltpu.make_async_copy(att.at[h], out_hbm.at[:, cols], out_sem.at[h])

    def recall(g):
        live = jnp.where(own_doc[:, 0:1] == ends()[0], 1.0, 0.0)
        state = jnp.concatenate([mem[g * (D // part) + n] for n in range(D // part)], axis=0)
        hi = state.astype(BF16)
        lo = (state - hi.astype(F32)).astype(BF16)
        both = jnp.concatenate([hi, lo], axis=1)
        q4 = jnp.concatenate([q_vm[4 * g + k] for k in range(4)], axis=0)
        r = jnp.dot(q4, both, preferred_element_type=F32)
        r = r[:, 0:D] + r[:, D:]
        for k in range(4):
            h = 4 * g + k
            rh = r[k * rows:(k + 1) * rows] * live
            mean = jnp.mean(rh * rh, axis=-1, keepdims=True)
            cols = pl.ds(pl.multiple_of(h * D, D), D)
            att[h] = att[h] + rh * lax.rsqrt(mean + 1e-6) * (gain_ref[:, cols] * mixing(h))
            out_copy(h).start()

    for d, same in others:
        doc_copy(d, same).start()
    for n, same in partners:
        part_copy(n, same).start()
    for g in range(GROUPS):
        send(g, 0)
    for d, same in others:
        doc_arrival(d, same).wait_recv()
    tail_state()
    hop(0, 0)
    masks()
    for h in range(HEADS):
        q_in(h).wait()
    smalls[1].wait()
    smalls[2].wait()
    hop(1, 0)
    hop(2, 0)
    hop(3, 0)
    part_memory()
    hop(0, 1)
    hop(1, 1)
    some(near, 0, 1)
    hop(2, 1)
    own_memory()
    some(near, 1, 3)
    hop(3, 1)
    some(near, 3, 4)
    hop(0, 2)
    some(near, 4, 5)
    hop(1, 2)
    some(near, 5, 6)
    hop(2, 2)
    some(near, 6, 7)
    hop(3, 2)
    some(near, 7, 8)
    for n, same in partners:
        memory_in(n, same).wait_recv()
    hop(0, 3)
    some(rest, 0, 2)
    some(recall, 0, 1)
    hop(1, 3)
    some(rest, 2, 4)
    some(recall, 1, 2)
    hop(2, 3)
    some(rest, 4, 6)
    some(recall, 2, 3)
    hop(3, 3)
    some(rest, 6, 8)
    some(recall, 3, 4)

    for h in range(half):
        for onward in (True, False):
            @pl.when(sent(h, onward))
            def _():
                for g in range(GROUPS):
                    ring(onward, g, h, 0).wait_send()
    for d, same in others:
        doc_copy(d, same).wait_send()
    for n, same in partners:
        part_copy(n, same).wait_send()
        memory_out(n, same).wait_send()
    state_along(1).wait_send()
    state_along(2).wait_send()
    state_across().wait_send()
    for h in range(HEADS):
        out_copy(h).wait()


def on_device(n_kv, n_seq, queries, keys, values, doc_ids, beta, lin_gain):
    rows = queries.shape[0]
    dma = pltpu.SemaphoreType.DMA
    part = D // 2
    return pl.pallas_call(
        functools.partial(kernel, n_kv, n_seq, rows),
        out_shape=jax.ShapeDtypeStruct((rows, HEADS * D), F32),
        in_specs=[pl.BlockSpec(memory_space=pltpu.HBM)] * 6,
        out_specs=pl.BlockSpec(memory_space=pl.ANY),
        scratch_shapes=[
            pltpu.VMEM((1, rows), jnp.int32),
            pltpu.SMEM((HEADS,), F32),
            pltpu.VMEM((1, HEADS * D), F32),
            pltpu.VMEM((HEADS, rows, D), BF16),
            pltpu.VMEM((GROUPS, rows, D), BF16),
            pltpu.VMEM((GROUPS, n_kv, D + rows, D), BF16),
            pltpu.VMEM((2, n_kv, 16, rows), BF16),
            pltpu.VMEM((n_kv, rows, rows), F32),
            pltpu.VMEM((HEADS // 2, 2 * rows, 1), F32),
            pltpu.VMEM((HEADS // 2, 2 * rows, 1), F32),
            pltpu.VMEM((HEADS // 2, 2 * rows, D), F32),
            pltpu.VMEM((HEADS, rows, D), F32),
            pltpu.VMEM((2 * GROUPS, part, D), F32),
            pltpu.VMEM((4, 2, part, D), F32),
            pltpu.VMEM((part + 8, D), F32),
            pltpu.VMEM((2, part + 8, D), F32),
            pltpu.VMEM((2, part, D), F32),
            pltpu.VMEM((2, part, D), F32),
            pltpu.VMEM((2, part, D), F32),
            pltpu.VMEM((2 * GROUPS, part, D), F32),
            dma((2 * GROUPS + HEADS + 3,)),
            dma((HEADS,)),
            dma((2, GROUPS, n_kv // 2)),
            dma((2, GROUPS, n_kv // 2)),
            dma((n_kv, 2)),
            dma((n_kv, 2)),
            dma((4, 2)),
            dma((4, 2)),
            dma((3,)),
            dma((3,)),
            dma((4, 2)),
            dma((4, 2)),
        ],
        compiler_params=pltpu.CompilerParams(
            collective_id=0, has_side_effects=True, vmem_limit_bytes=60 * 1024 * 1024),
    )(queries, keys, values, doc_ids.reshape(1, rows), beta, lin_gain.reshape(1, HEADS * D))


def solution(mesh):
    split = P(("dp", "seq", "kv"))
    rows = P(("dp", "seq", "kv"), None)
    return jax.shard_map(
        functools.partial(on_device, mesh.shape["kv"], mesh.shape["seq"]),
        mesh=mesh, in_specs=(rows, rows, rows, split, P(), P()), out_specs=rows, check_vma=False)
```

time: 52.1 us -> 46.9 us (0.900)
  the two profiles are of different devices: /device:TPU:4 before, /device:TPU:1 now
where the time goes in v3:
time: 46.9 us; the launch traced here: 46.7 us
  Pallas kernels  44.4 us (95%)
  local copies, waits for them, and re-layouts  2.3 us (5%)
    pallas_call x1, Pallas kernels, on_device(): pl.pallas_call(functools.partial(kernel, n_kv, n_seq, rows), out_shape=ja...  44.4 us
    unnamed x1, local copies, waits for them, and re-layouts  2.3 us

profile of v3, /device:TPU:1, one launch (start us, length us, event | category | flops | bytes accessed | tf_op | source)
XLA Modules:
  0.0 46.7 jit_solution(13574046614838179202)
XLA Ops:
  0.0 44.4 %shard_map.64 = f32[128,2048]{1,0:T(8,128)} custom-call(bf16[128,2048]{1,0:T(8,128)(2,1)} %q_hbm.1, bf16[128,512]{1,0:T(8,128)(2,1)} %k_hbm.1, bf16[128,512]{1,0:T(8,128)(2,1)} %v_hbm.1, s32[1,128]{1,0:T(1,128)} %bitcast.3, f32[16]{0:T(128)} %beta_hbm.1, f32[1,2048]{1,0:T(1,128)} %bitcast.2), custom_call_target="tpu_custom_call" | custom-call | tf_op jit(solution)/shard_map/pallas_call | solution.py:386
  44.4 2.3 %copy.8 = f32[128,2048]{1,0:T(8,128)} copy(f32[128,2048]{1,0:T(8,128)} %shard_map.64) | data formatting | bytes 2097152

commit v4 on v3

--- a/solution.py
+++ b/solution.py
@@ -16,6 +16,7 @@
 BF16 = jnp.bfloat16
 NEG = -1e30
 NEAR = (-2, -1, 0, 1, 2)
+BACK = (-2, -1, 0)
 FAR = (-3, 3, 4)
 
 
@@ -123,40 +124,39 @@
             send_sem=p_send.at[n, c], recv_sem=p_recv.at[n, c],
             device_id={"kv": me, "seq": other}, device_id_type=MESH)
 
-    def span(h, onward):
-        if h < half - 1:
+    def span(h, onward, whole):
+        if h < half - 1 and whole:
             return pl.ds(0, D + rows)
         return pl.ds(0, D) if onward else pl.ds(D, rows)
 
-    def ring(onward, g, h, ahead):
+    def ring(onward, g, h, ahead, whole=True):
         blk = away(-h - ahead if onward else h + ahead)
-        ref = kv.at[g, blk, span(h, onward)]
+        ref = kv.at[g, blk, span(h, onward, whole)]
         t = 0 if onward else 1
         return pltpu.make_async_remote_copy(
             src_ref=ref, dst_ref=ref, send_sem=ring_send.at[t, g, h], recv_sem=ring_recv.at[t, g, h],
             device_id={"kv": away(1 if onward else -1)}, device_id_type=MESH)
 
-    def sent(h, onward):
-        return (me >= h) & (me < n_kv - 1) if onward else away(h) < half
-
-    def arrives(h, onward):
-        return me > h if onward else away(h + 1) < half
+    def legs(h, ahead):
+        right_on = (me >= h) & (me < n_kv - 1) if ahead == 0 else me > h
+        blk = away(h + ahead)
+        if h == half - 1:
+            return ((True, right_on, True), (False, blk < half, True))
+        return ((True, right_on, True), (False, blk < half - 1, True), (False, blk == half - 1, False))
 
     def send(g, h):
-        for onward in (True, False):
-            @pl.when(sent(h, onward))
+        for onward, on, whole in legs(h, 0):
+            @pl.when(on)
             def _():
-                ring(onward, g, h, 0).start()
+                ring(onward, g, h, 0, whole).start()
 
     def hop(g, h):
-        for onward in (True, False):
-            @pl.when(arrives(h, onward))
+        for onward, on, whole in legs(h, 1):
+            @pl.when(on)
             def _():
-                ring(onward, g, h, 1).wait_recv()
-            if h + 1 < half:
-                @pl.when(sent(h + 1, onward))
-                def _():
-                    ring(onward, g, h + 1, 0).start()
+                ring(onward, g, h, 1, whole).wait_recv()
+        if h + 1 < half:
+            send(g, h + 1)
 
     def state_along(step):
         return pltpu.make_async_remote_copy(
@@ -216,22 +216,26 @@
         v = jnp.concatenate([kv[i // 2, away(o), D:D + rows] for o in offs], axis=0)
         return jnp.dot(p.astype(BF16), v, preferred_element_type=F32)
 
-    def near(i):
-        s = scores(i, NEAR)
+    def first_pass(i, offs):
+        s = scores(i, offs)
         m = jnp.max(s, axis=-1, keepdims=True)
         p = jnp.exp2((s - m) * scale)
         top[i] = m
         total[i] = jnp.sum(p, axis=-1, keepdims=True)
-        acc[i] = weighted(i, NEAR, p)
-
-    def far(i):
-        s = scores(i, FAR)
+        acc[i] = weighted(i, offs, p)
+
+    def near(i):
+        pl.when(me < n_kv - 2)(lambda: first_pass(i, BACK))
+        pl.when(me >= n_kv - 2)(lambda: first_pass(i, NEAR))
+
+    def far(i, offs):
+        s = scores(i, offs)
         old = top[i]
         m = jnp.maximum(old, jnp.max(s, axis=-1, keepdims=True))
         p = jnp.exp2((s - m) * scale)
         kept = jnp.exp2((old - m) * scale)
         norm = total[i] * kept + jnp.sum(p, axis=-1, keepdims=True)
-        o = (acc[i] * kept + weighted(i, FAR, p)) / norm
+        o = (acc[i] * kept + weighted(i, offs, p)) / norm
         att[2 * i] = o[:rows] * (1.0 - mixing(2 * i))
         att[2 * i + 1] = o[rows:] * (1.0 - mixing(2 * i + 1))
 
@@ -239,10 +243,6 @@
         o = acc[i] / total[i]
         att[2 * i] = o[:rows] * (1.0 - mixing(2 * i))
         att[2 * i + 1] = o[rows:] * (1.0 - mixing(2 * i + 1))
-
-    def rest(i):
-        pl.when(me >= 3)(lambda: far(i))
-        pl.when(me < 3)(lambda: settle(i))
 
     def some(f, start, stop):
         pl.loop(start, stop)(f)
@@ -332,41 +332,67 @@
     part_memory()
     hop(0, 1)
     hop(1, 1)
-    some(near, 0, 1)
     hop(2, 1)
-    own_memory()
-    some(near, 1, 3)
     hop(3, 1)
-    some(near, 3, 4)
-    hop(0, 2)
-    some(near, 4, 5)
-    hop(1, 2)
-    some(near, 5, 6)
-    hop(2, 2)
-    some(near, 6, 7)
-    hop(3, 2)
-    some(near, 7, 8)
-    for n, same in partners:
-        memory_in(n, same).wait_recv()
-    hop(0, 3)
-    some(rest, 0, 2)
-    some(recall, 0, 1)
-    hop(1, 3)
-    some(rest, 2, 4)
-    some(recall, 1, 2)
-    hop(2, 3)
-    some(rest, 4, 6)
-    some(recall, 2, 3)
-    hop(3, 3)
-    some(rest, 6, 8)
-    some(recall, 3, 4)
+
+    @pl.loop(0, HEADS // 2)
+    def _(i):
+        near(i)
+
+        @pl.when(i == 0)
+        def _():
+            own_memory()
+            hop(0, 2)
+
+        @pl.when(i == 2)
+        def _():
+            hop(1, 2)
+
+        @pl.when(i == 4)
+        def _():
+            hop(2, 2)
+
+        @pl.when(i == 6)
+        def _():
+            hop(3, 2)
+
+    @pl.when(me < half)
+    def _():
+        @pl.loop(0, HEADS // 2)
+        def _(i):
+            pl.when(me == half - 1)(lambda: far(i, FAR[:1]))
+            pl.when(me < half - 1)(lambda: settle(i))
+
+        for n, same in partners:
+            memory_in(n, same).wait_recv()
+        some(recall, 0, GROUPS)
+
+    @pl.when(me >= half)
+    def _():
+        @pl.loop(0, GROUPS)
+        def _(g):
+            for ahead in range(GROUPS):
+                @pl.when(g == ahead)
+                def _():
+                    hop(ahead, half - 1)
+
+            @pl.loop(2 * g, 2 * g + 2)
+            def _(i):
+                far(i, FAR)
+
+            @pl.when(g == 0)
+            def _():
+                for n, same in partners:
+                    memory_in(n, same).wait_recv()
+
+            recall(g)
 
     for h in range(half):
-        for onward in (True, False):
-            @pl.when(sent(h, onward))
+        for onward, on, whole in legs(h, 0):
+            @pl.when(on)
             def _():
                 for g in range(GROUPS):
-                    ring(onward, g, h, 0).wait_send()
+                    ring(onward, g, h, 0, whole).wait_send()
     for d, same in others:
         doc_copy(d, same).wait_send()
     for n, same in partners:

time: 46.9 us -> 46 us (0.981)
  Pallas kernels: 44.4 us -> 43.4 us
    pallas_call x1, Pallas kernels: 44.4 us -> 43.4 us  [on_device(): pl.pallas_call(functools.partial(kernel, n_kv, n_seq, rows), out_shape=ja...]
where the time goes in v4:
time: 46 us; the launch traced here: 45.7 us
  Pallas kernels  43.4 us (94%)
  local copies, waits for them, and re-layouts  2.3 us (5%)
    pallas_call x1, Pallas kernels, on_device(): pl.pallas_call(functools.partial(kernel, n_kv, n_seq, rows), out_shape=ja...  43.4 us
    unnamed x1, local copies, waits for them, and re-layouts  2.3 us

profile of v4, /device:TPU:1, one launch (start us, length us, event | category | flops | bytes accessed | tf_op | source)
XLA Modules:
  0.0 45.7 jit_solution(13024338292253254235)
XLA Ops:
  0.0 43.4 %shard_map.64 = f32[128,2048]{1,0:T(8,128)} custom-call(bf16[128,2048]{1,0:T(8,128)(2,1)} %q_hbm.1, bf16[128,512]{1,0:T(8,128)(2,1)} %k_hbm.1, bf16[128,512]{1,0:T(8,128)(2,1)} %v_hbm.1, s32[1,128]{1,0:T(1,128)} %bitcast.3, f32[16]{0:T(128)} %beta_hbm.1, f32[1,2048]{1,0:T(1,128)} %bitcast.2), custom_call_target="tpu_custom_call" | custom-call | tf_op jit(solution)/shard_map/pallas_call | solution.py:412
  43.4 2.3 %copy.8 = f32[128,2048]{1,0:T(8,128)} copy(f32[128,2048]{1,0:T(8,128)} %shard_map.64) | data formatting | bytes 2097152

commit v5 on v4

--- a/solution.py
+++ b/solution.py
@@ -43,6 +43,7 @@
     barrier = pltpu.get_barrier_semaphore()
     for d in range(1, n_kv):
         pl.semaphore_signal(barrier, inc=1, device_id={"kv": away(d)}, device_id_type=MESH)
+    for d in (1, 2, -1, -2):
         pl.semaphore_signal(barrier, inc=1, device_id={"kv": away(d), "seq": other}, device_id_type=MESH)
     for d in (other, along(1), along(2), along(-1), along(-2)):
         pl.semaphore_signal(barrier, inc=1, device_id={"seq": d}, device_id_type=MESH)
@@ -65,10 +66,6 @@
         k_in(g).start()
     for g in range(GROUPS):
         v_in(g).start()
-    smalls[1].start()
-    smalls[2].start()
-    for h in range(HEADS):
-        q_in(h).start()
     smalls[0].wait()
     docs[core, me] = jnp.broadcast_to(docs_ref[...].astype(BF16), (16, rows))
     for j in range(half, n_kv):
@@ -87,7 +84,7 @@
         p = jnp.dot(kv[g, me, 0:D] * ending, kv[g, me, D:D + rows], preferred_element_type=F32)
         for n in range(D // part):
             p_own[g * (D // part) + n] = p[n * part:(n + 1) * part]
-    pl.semaphore_wait(barrier, 2 * (n_kv - 1) + 5)
+    pl.semaphore_wait(barrier, n_kv - 1 + 9)
 
     def core_at(same):
         return (core, seq) if same else (1 - core, other)
@@ -95,19 +92,23 @@
     others = [(d, same) for d in range(n_kv) for same in (True, False) if d or not same]
     partners = [(n, same) for n in range(4) for same in (True, False) if n < 3 or not same]
 
-    def doc_copy(d, same):
-        c, s = core_at(same)
+    def doc_copy(d):
         ref = docs.at[core, me]
         return pltpu.make_async_remote_copy(
-            src_ref=ref, dst_ref=ref, send_sem=doc_send.at[d, c], recv_sem=doc_recv.at[d, core],
-            device_id={"kv": away(d), "seq": s}, device_id_type=MESH)
-
-    def doc_arrival(d, same):
-        c, s = core_at(same)
-        ref = docs.at[c, away(-d)]
-        return pltpu.make_async_remote_copy(
-            src_ref=ref, dst_ref=ref, send_sem=doc_send.at[d, c], recv_sem=doc_recv.at[d, c],
-            device_id={"kv": away(d), "seq": other}, device_id_type=MESH)
+            src_ref=ref, dst_ref=ref, send_sem=doc_send.at[d], recv_sem=doc_recv.at[d],
+            device_id={"kv": away(d)}, device_id_type=MESH)
+
+    def doc_arrival(d):
+        ref = docs.at[core, away(-d)]
+        return pltpu.make_async_remote_copy(
+            src_ref=ref, dst_ref=ref, send_sem=doc_send.at[d], recv_sem=doc_recv.at[d],
+            device_id={"kv": away(d)}, device_id_type=MESH)
+
+    def doc_exchange(c):
+        ref = docs.at[c]
+        return pltpu.make_async_remote_copy(
+            src_ref=ref, dst_ref=ref, send_sem=doc_send.at[0], recv_sem=doc_recv.at[0],
+            device_id={"seq": other}, device_id_type=MESH)
 
     def part_copy(n, same):
         c, s = core_at(same)
@@ -311,14 +312,20 @@
             att[h] = att[h] + rh * lax.rsqrt(mean + 1e-6) * (gain_ref[:, cols] * mixing(h))
             out_copy(h).start()
 
-    for d, same in others:
-        doc_copy(d, same).start()
     for n, same in partners:
         part_copy(n, same).start()
+    for d in range(1, n_kv):
+        doc_copy(d).start()
     for g in range(GROUPS):
         send(g, 0)
-    for d, same in others:
-        doc_arrival(d, same).wait_recv()
+    smalls[1].start()
+    smalls[2].start()
+    for h in range(HEADS):
+        q_in(h).start()
+    for d in range(1, n_kv):
+        doc_arrival(d).wait_recv()
+    doc_exchange(core).start()
+    doc_exchange(1 - core).wait_recv()
     tail_state()
     hop(0, 0)
     masks()
@@ -363,9 +370,11 @@
             pl.when(me == half - 1)(lambda: far(i, FAR[:1]))
             pl.when(me < half - 1)(lambda: settle(i))
 
-        for n, same in partners:
-            memory_in(n, same).wait_recv()
-        some(recall, 0, GROUPS)
+        for n in (3, 0, 1, 2):
+            for k, same in partners:
+                if k == n:
+                    memory_in(k, same).wait_recv()
+            recall(lax.rem(me + (GROUPS - 1, 1, 2, 0)[n], GROUPS))
 
     @pl.when(me >= half)
     def _():
@@ -393,8 +402,9 @@
             def _():
                 for g in range(GROUPS):
                     ring(onward, g, h, 0, whole).wait_send()
-    for d, same in others:
-        doc_copy(d, same).wait_send()
+    for d in range(1, n_kv):
+        doc_copy(d).wait_send()
+    doc_exchange(core).wait_send()
     for n, same in partners:
         part_copy(n, same).wait_send()
         memory_out(n, same).wait_send()
@@ -439,8 +449,8 @@
             dma((HEADS,)),
             dma((2, GROUPS, n_kv // 2)),
             dma((2, GROUPS, n_kv // 2)),
-            dma((n_kv, 2)),
-            dma((n_kv, 2)),
+            dma((n_kv,)),
+            dma((n_kv,)),
             dma((4, 2)),
             dma((4, 2)),
             dma((3,)),

time: 46 us -> 45.3 us (0.985)
  Pallas kernels: 43.4 us -> 42.4 us
    pallas_call x1, Pallas kernels: 43.4 us -> 42.4 us  [on_device(): pl.pallas_call(functools.partial(kernel, n_kv, n_seq, rows), out_shape=ja...]
where the time goes in v5:
time: 45.3 us; the launch traced here: 44.7 us
  Pallas kernels  42.4 us (94%)
  local copies, waits for them, and re-layouts  2.3 us (5%)
    pallas_call x1, Pallas kernels, on_device(): pl.pallas_call(functools.partial(kernel, n_kv, n_seq, rows), out_shape=ja...  42.4 us
    unnamed x1, local copies, waits for them, and re-layouts  2.3 us

profile of v5, /device:TPU:1, one launch (start us, length us, event | category | flops | bytes accessed | tf_op | source)
XLA Modules:
  0.0 44.7 jit_solution(18270373617610663368)
XLA Ops:
  0.0 42.4 %shard_map.64 = f32[128,2048]{1,0:T(8,128)} custom-call(bf16[128,2048]{1,0:T(8,128)(2,1)} %q_hbm.1, bf16[128,512]{1,0:T(8,128)(2,1)} %k_hbm.1, bf16[128,512]{1,0:T(8,128)(2,1)} %v_hbm.1, s32[1,128]{1,0:T(1,128)} %bitcast.3, f32[16]{0:T(128)} %beta_hbm.1, f32[1,2048]{1,0:T(1,128)} %bitcast.2), custom_call_target="tpu_custom_call" | custom-call | tf_op jit(solution)/shard_map/pallas_call | solution.py:422
  42.4 2.3 %copy.8 = f32[128,2048]{1,0:T(8,128)} copy(f32[128,2048]{1,0:T(8,128)} %shard_map.64) | data formatting | bytes 2097152

commit v6 on v5

--- a/solution.py
+++ b/solution.py
@@ -348,8 +348,8 @@
 
         @pl.when(i == 0)
         def _():
+            hop(0, 2)
             own_memory()
-            hop(0, 2)
 
         @pl.when(i == 2)
         def _():
@@ -387,7 +387,8 @@
 
             @pl.loop(2 * g, 2 * g + 2)
             def _(i):
-                far(i, FAR)
+                pl.when(me == half)(lambda: far(i, FAR[::2]))
+                pl.when(me > half)(lambda: far(i, FAR))
 
             @pl.when(g == 0)
             def _():

time: 45.3 us -> 44.9 us (level)
  no operation moved by 1% of the time
where the time goes in v6:
time: 44.9 us; the launch traced here: 44.7 us
  Pallas kernels  42.4 us (94%)
  local copies, waits for them, and re-layouts  2.3 us (5%)
    pallas_call x1, Pallas kernels, on_device(): pl.pallas_call(functools.partial(kernel, n_kv, n_seq, rows), out_shape=ja...  42.4 us
    unnamed x1, local copies, waits for them, and re-layouts  2.3 us

profile of v6, /device:TPU:1, one launch (start us, length us, event | category | flops | bytes accessed | tf_op | source)
XLA Modules:
  0.0 44.7 jit_solution(1203550766928407509)
XLA Ops:
  0.0 42.4 %shard_map.64 = f32[128,2048]{1,0:T(8,128)} custom-call(bf16[128,2048]{1,0:T(8,128)(2,1)} %q_hbm.1, bf16[128,512]{1,0:T(8,128)(2,1)} %k_hbm.1, bf16[128,512]{1,0:T(8,128)(2,1)} %v_hbm.1, s32[1,128]{1,0:T(1,128)} %bitcast.3, f32[16]{0:T(128)} %beta_hbm.1, f32[1,2048]{1,0:T(1,128)} %bitcast.2), custom_call_target="tpu_custom_call" | custom-call | tf_op jit(solution)/shard_map/pallas_call | solution.py:423
  42.4 2.3 %copy.8 = f32[128,2048]{1,0:T(8,128)} copy(f32[128,2048]{1,0:T(8,128)} %shard_map.64) | data formatting | bytes 2097152

commit v7 on v6

--- a/solution.py
+++ b/solution.py
@@ -90,7 +90,7 @@
         return (core, seq) if same else (1 - core, other)
 
     others = [(d, same) for d in range(n_kv) for same in (True, False) if d or not same]
-    partners = [(n, same) for n in range(4) for same in (True, False) if n < 3 or not same]
+    partners = [(n, same) for n in (2, 0, 1, 3) for same in (True, False) if n < 3 or not same]
 
     def doc_copy(d):
         ref = docs.at[core, me]
@@ -269,8 +269,8 @@
         (even, _, even_last), (odd, odd_first, odd_last) = states
         c_own[0:part] = odd + jnp.where(even_last == odd_last, even, 0.0)
         c_own[part:part + 8] = jnp.broadcast_to(odd_last, (8, D))
+        state_along(2).start()
         state_along(1).start()
-        state_along(2).start()
         x_own[1] = jnp.where(even_last == odd_first, even, 0.0)
 
     def part_memory():

time: 44.9 us -> 45.2 us (level)
  no operation moved by 1% of the time
where the time goes in v7:
time: 45.2 us; the launch traced here: 45 us
  Pallas kernels  42.7 us (94%)
  local copies, waits for them, and re-layouts  2.3 us (5%)
    pallas_call x1, Pallas kernels, on_device(): pl.pallas_call(functools.partial(kernel, n_kv, n_seq, rows), out_shape=ja...  42.7 us
    unnamed x1, local copies, waits for them, and re-layouts  2.3 us

profile of v7, /device:TPU:1, one launch (start us, length us, event | category | flops | bytes accessed | tf_op | source)
XLA Modules:
  0.0 45.0 jit_solution(6641635732542912149)
XLA Ops:
  0.0 42.7 %shard_map.64 = f32[128,2048]{1,0:T(8,128)} custom-call(bf16[128,2048]{1,0:T(8,128)(2,1)} %q_hbm.1, bf16[128,512]{1,0:T(8,128)(2,1)} %k_hbm.1, bf16[128,512]{1,0:T(8,128)(2,1)} %v_hbm.1, s32[1,128]{1,0:T(1,128)} %bitcast.3, f32[16]{0:T(128)} %beta_hbm.1, f32[1,2048]{1,0:T(1,128)} %bitcast.2), custom_call_target="tpu_custom_call" | custom-call | tf_op jit(solution)/shard_map/pallas_call | solution.py:423
  42.7 2.3 %copy.8 = f32[128,2048]{1,0:T(8,128)} copy(f32[128,2048]{1,0:T(8,128)} %shard_map.64) | data formatting | bytes 2097152
